TPU v7x, 256 devices: a whole 4x4x8 slice. The times are simulated.
256 devices in a mesh: seq: 64 (over x_hi, y, z), kvh: 4 (over x_lo, core).
Axes of the slice: x: 4 (x_hi: 2, x_lo: 2; x = x_hi * 2 + x_lo), y: 4, z: 8, core: 2. Of those that a mesh axis runs over, the one named last changes fastest.
Arguments:
- queries: bfloat16 [32768, 4096], P(('seq', 'kvh')), may hold values from -5 to 5
- key_rows: bfloat16 [32768, 2048], P(('seq', 'kvh')), may hold values from -6 to 6
- value_rows: bfloat16 [32768, 2048], P(('seq', 'kvh')), may hold values from -6 to 6
- grad_out: bfloat16 [32768, 4096], P(('seq', 'kvh')), may hold values from -6 to 6
Outputs:
- attended: bfloat16 [32768, 4096], P(('seq', 'kvh'))
- grad_queries: bfloat16 [32768, 4096], P(('seq', 'kvh'))
- grad_keys: bfloat16 [32768, 2048], P(('seq', 'kvh'))
- grad_values: bfloat16 [32768, 2048], P(('seq', 'kvh'))
All inputs are finite; a program needn't handle non-finite values.
Results may differ from a plain program's by a relative error of at most 0.012.
Values may be sent and summed in bfloat16 or wider, within the bound.
A program may use at most 128 MiB of HBM per device.

v0:
```python
import math

import jax
import jax.numpy as jnp
from jax import lax
from jax.sharding import PartitionSpec as P

HEAD_DIM = 128
WINDOW = 1024


score_scale = 168.0 ** (-0.5)


def as_sent(shard):

    def short(part):
        return part.astype(jnp.bfloat16) if part.dtype == jnp.float32 else part

    return jax.tree.map(short, shard)


def passed_along(value, axis, steps):
    count = lax.axis_size(axis)
    first, last = (max(0, -steps), min(count, count - steps))
    return lax.ppermute(value, axis, [(source, source + steps) for source in range(first, last)])


def head_loop(queries, grad_out, window_keys, window_values, query_pos, key_pos):
    row_count = queries.shape[0]
    key_count = window_keys.shape[0]
    kv_count = window_keys.shape[1] // HEAD_DIM
    allowed = (
        (key_pos[None, :] <= query_pos[:, None])
        & (query_pos[:, None] - key_pos[None, :] < WINDOW)
        & (key_pos[None, :] >= 0)
    )

    def one_head(kv_head, totals):
        attended, grad_q, grad_k, grad_v = totals
        q_cols = kv_head * (2 * HEAD_DIM)
        k_cols = kv_head * HEAD_DIM
        q_head = lax.dynamic_slice_in_dim(queries, q_cols, 2 * HEAD_DIM, 1).reshape(
            row_count, 2, HEAD_DIM
        )
        o_head = lax.dynamic_slice_in_dim(grad_out, q_cols, 2 * HEAD_DIM, 1).reshape(
            row_count, 2, HEAD_DIM
        )
        k_head = lax.dynamic_slice_in_dim(window_keys, k_cols, HEAD_DIM, 1)
        v_head = lax.dynamic_slice_in_dim(window_values, k_cols, HEAD_DIM, 1)
        scores = (
            jnp.einsum("rhd,kd->hrk", q_head, k_head, preferred_element_type=jnp.float32)
            * score_scale
        )
        scores = jnp.where(allowed[None], scores, -jnp.inf)
        row_max = jnp.max(scores, axis=-1, keepdims=True)
        exponent = jnp.exp(scores - row_max)
        weights = exponent / jnp.sum(exponent, axis=-1, keepdims=True)
        weights_low = weights.astype(jnp.bfloat16)
        out_head = jnp.einsum(
            "hrk,kd->rhd", weights_low, v_head, preferred_element_type=jnp.float32
        )
        grad_weights = jnp.einsum("rhd,kd->hrk", o_head, v_head, preferred_element_type=jnp.float32)
        row_delta = jnp.sum(weights * grad_weights, axis=-1, keepdims=True)
        grad_scores = (weights * (grad_weights - row_delta)).astype(jnp.bfloat16)
        dq_head = (
            jnp.einsum("hrk,kd->rhd", grad_scores, k_head, preferred_element_type=jnp.float32)
            * score_scale
        )
        dk_head = (
            jnp.einsum("hrk,rhd->kd", grad_scores, q_head, preferred_element_type=jnp.float32)
            * score_scale
        )
        dv_head = jnp.einsum("hrk,rhd->kd", weights_low, o_head, preferred_element_type=jnp.float32)
        attended = lax.dynamic_update_slice_in_dim(
            attended, out_head.reshape(row_count, 2 * HEAD_DIM).astype(jnp.bfloat16), q_cols, 1
        )
        grad_q = lax.dynamic_update_slice_in_dim(
            grad_q, dq_head.reshape(row_count, 2 * HEAD_DIM).astype(jnp.bfloat16), q_cols, 1
        )
        grad_k = lax.dynamic_update_slice_in_dim(grad_k, dk_head, k_cols, 1)
        grad_v = lax.dynamic_update_slice_in_dim(grad_v, dv_head, k_cols, 1)
        return (attended, grad_q, grad_k, grad_v)

    initial = (
        jnp.zeros(queries.shape, jnp.bfloat16),
        jnp.zeros(queries.shape, jnp.bfloat16),
        jnp.zeros((key_count, window_keys.shape[1]), jnp.float32),
        jnp.zeros((key_count, window_keys.shape[1]), jnp.float32),
    )
    return lax.fori_loop(0, kv_count, one_head, initial)


def window_core(queries, key_rows, value_rows, grad_out, shard_index, fetch_pair, give_back):
    row_count = queries.shape[0]
    back_count = -(-WINDOW // row_count)
    pieces = [fetch_pair((key_rows, value_rows), offset) for offset in range(back_count, 0, -1)]
    window_keys = jnp.concatenate([piece[0] for piece in pieces] + [key_rows], axis=0)
    window_values = jnp.concatenate([piece[1] for piece in pieces] + [value_rows], axis=0)
    query_pos = shard_index * row_count + jnp.arange(row_count, dtype=jnp.int32)
    key_pos = (
        shard_index * row_count
        - back_count * row_count
        + jnp.arange((back_count + 1) * row_count, dtype=jnp.int32)
    )
    own_start = back_count * row_count
    block_rows = math.gcd(row_count, WINDOW // 8)
    key_span = WINDOW + block_rows
    grad_kwin = jnp.zeros(window_keys.shape, jnp.float32)
    grad_vwin = jnp.zeros(window_values.shape, jnp.float32)
    key_first = own_start - WINDOW
    result = head_loop(queries, grad_out, window_keys, window_values, query_pos, key_pos)
    attended_parts = result[0]
    grad_q_parts = result[1]
    grad_kwin = grad_kwin.at[key_first : key_first + key_span].add(result[2])
    grad_vwin = grad_vwin.at[key_first : key_first + key_span].add(result[3])
    grad_k = grad_kwin[own_start:]
    grad_v = grad_vwin[own_start:]
    for offset in range(1, back_count + 1):
        start_row = (back_count - offset) * row_count
        returned = give_back(
            (
                grad_kwin[start_row : start_row + row_count],
                grad_vwin[start_row : start_row + row_count],
            ),
            -offset,
        )
        grad_k = grad_k + returned[0]
        grad_v = grad_v + returned[1]
    return (attended_parts, grad_q_parts, grad_k.astype(jnp.bfloat16), grad_v.astype(jnp.bfloat16))


def body(queries, key_rows, value_rows, grad_out):

    def fetch_all(pair, offset):
        return jax.tree.map(
            lambda part, own: part.astype(own.dtype),
            passed_along(as_sent(pair), ("seq", "kvh"), offset),
            pair,
        )

    def return_all(pair, offset):
        return passed_along(pair, ("seq", "kvh"), offset)

    shard_index = lax.axis_index(("seq", "kvh"))
    results = window_core(
        queries, key_rows, value_rows, grad_out, shard_index, fetch_all, return_all
    )
    return (results[0], results[1], results[2], results[3])


def solution(mesh):
    return jax.shard_map(
        body,
        mesh=mesh,
        in_specs=(
            P(("seq", "kvh"), None),
            P(("seq", "kvh"), None),
            P(("seq", "kvh"), None),
            P(("seq", "kvh"), None),
        ),
        out_specs=(
            P(("seq", "kvh"), None),
            P(("seq", "kvh"), None),
            P(("seq", "kvh"), None),
            P(("seq", "kvh"), None),
        ),
        check_vma=False,
    )
```

profile of v0, /device:TPU:216, one launch (start us, length us, event | category | flops | bytes accessed | tf_op | source)
XLA Modules:
  0.0 1021.0 jit_solution(1511458429021108816)
XLA Ops:
  5.9 3.4 collective-permute-start.6
  9.4 3.6 collective-permute-start.10
  13.0 7.0 collective-permute-start.9
  20.0 9.8 collective-permute-done.8
  31.8 23.1 %collective-permute-done.9 = bf16[128,2048]{1,0:T(8,128)(2,1)} collective-permute-done((bf16[128,2048]{1,0:T(8,128)(2,1)}, bf16[128,2048]{1,0:T(8,128)(2,1)}, u32[]{:S(2)}, u32[]{:S(2)}) %collective-permute-start.9) | collective-permute-done | bytes 524320 | tf_op jit(solution)/shard_map/ppermute | solution.py:26
  54.9 4.4 collective-permute-start.12
  60.3 39.1 %collective-permute-start.13 = (bf16[128,2048]{1,0:T(8,128)(2,1)}, bf16[128,2048]{1,0:T(8,128)(2,1)S(1)}, u32[]{:S(2)}, u32[]{:S(2)}) collective-permute-start(bf16[128,2048]{1,0:T(8,128)(2,1)} %param.15), channel_id=1, source_target_pairs={{0,3},{1,4},{2,5},{3,6},{4,7},{5,8},{6,9},{7,10},{8,11},{9,12},{10... | collective-permute-start | bytes 1572872 | tf_op jit(solution)/shard_map/ppermute | solution.py:26
  99.5 7.9 collective-permute-done.11
  111.4 21.2 %collective-permute-start.2 = (bf16[128,2048]{0,1:T(8,128)(2,1)S(1)}, bf16[128,2048]{0,1:T(8,128)(2,1)S(1)}, u32[]{:S(2)}, u32[]{:S(2)}) collective-permute-start(bf16[128,2048]{0,1:T(8,128)(2,1)S(1)} %copy.31), channel_id=1, source_target_pairs={{0,6},{1,7},{2,8},{3,9},{4,10},{5,11},{6,12},{7,13},{8,14},{9,15},... | collective-permute-start | bytes 1572872 | tf_op jit(solution)/shard_map/ppermute | solution.py:26
  132.7 5.0 collective-permute-done.14
  137.7 9.8 collective-permute-start
  147.6 17.4 %collective-permute-done.15 = bf16[128,2048]{1,0:T(8,128)(2,1)S(1)} collective-permute-done((bf16[128,2048]{1,0:T(8,128)(2,1)S(1)}, bf16[128,2048]{1,0:T(8,128)(2,1)S(1)}, u32[]{:S(2)}, u32[]{:S(2)}) %collective-permute-start.15) | collective-permute-done | bytes 524320 | tf_op jit(solution)/shard_map/ppermute | solution.py:26
  167.0 3.0 collective-permute-done
  169.9 4.0 collective-permute-start.3
  174.0 13.6 %collective-permute-done.1 = bf16[128,2048]{0,1:T(8,128)(2,1)S(1)} collective-permute-done((bf16[128,2048]{0,1:T(8,128)(2,1)S(1)}, bf16[128,2048]{0,1:T(8,128)(2,1)S(1)}, u32[]{:S(2)}, u32[]{:S(2)}) %collective-permute-start.1) | collective-permute-done | bytes 524320 | tf_op jit(solution)/shard_map/ppermute | solution.py:26
  187.6 3.6 collective-permute-start.4
  191.4 36.7 %collective-permute-start.5 = (bf16[128,2048]{0,1:T(8,128)(2,1)S(1)}, bf16[128,2048]{0,1:T(8,128)(2,1)S(1)}, u32[]{:S(2)}, u32[]{:S(2)}) collective-permute-start(bf16[128,2048]{0,1:T(8,128)(2,1)S(1)} %copy.31), channel_id=1, source_target_pairs={{0,3},{1,4},{2,5},{3,6},{4,7},{5,8},{6,9},{7,10},{8,11},{9,12},{10... | collective-permute-start | bytes 1572872 | tf_op jit(solution)/shard_map/ppermute | solution.py:26
  228.5 6.3 collective-permute-done.5
  238.7 4.8 broadcast.90.clone
  243.6 4.9 broadcast.90
  248.4 225.1 %while.24 = (s32[]{:T(128)}, bf16[128,4096]{1,0:T(8,128)(2,1)}, bf16[128,4096]{1,0:T(8,128)(2,1)S(1)}, f32[1152,2048]{1,0:T(8,128)}, f32[1152,2048]{1,0:T(8,128)...) while((s32[]{:T(128)}, bf16[128,4096]{1,0:T(8,128)(2,1)}, ...), condition=%wide.region_4.5_spmd.clone, body=%wide.region_0.4_spmd.clone.sunk | while | flops 611159680 | bytes 12795301 | solution.py:91
  259.7 2.8 fusion.96
  273.7 2.8 fusion.96
  287.8 2.8 fusion.96
  301.9 2.8 fusion.96
  316.0 2.8 fusion.96
  330.0 2.8 fusion.96
  344.0 2.8 fusion.96
  358.1 2.8 fusion.96
  372.2 2.8 fusion.96
  386.3 2.8 fusion.96
  400.4 2.8 fusion.96
  414.4 2.8 fusion.96
  428.5 2.8 fusion.96
  442.6 2.8 fusion.96
  456.6 2.8 fusion.96
  470.7 2.8 fusion.96
  473.5 7.1 fusion.47
  480.6 19.9 %collective-permute-start.24 = (f32[128,2048]{1,0:T(8,128)S(1)}, f32[128,2048]{1,0:T(8,128)S(1)}, u32[]{:S(2)}, u32[]{:S(2)}) collective-permute-start(f32[128,2048]{1,0:T(8,128)S(1)} %get-tuple-element.299), channel_id=1, source_target_pairs={{1,0},{2,1},{3,2},{4,3},{5,4},{6,5},{7,6},{8,7},{9,8},{10,9},{11,1... | collective-permute-start | bytes 3145736 | tf_op jit(solution)/shard_map/ppermute | solution.py:26
  502.5 9.8 collective-permute-start.29
  512.4 5.1 collective-permute-start.28
  519.4 13.3 %collective-permute-start.26 = (f32[128,2048]{1,0:T(8,128)}, f32[128,2048]{1,0:T(8,128)S(1)}, u32[]{:S(2)}, u32[]{:S(2)}) collective-permute-start(f32[128,2048]{1,0:T(8,128)} %get-tuple-element.304), channel_id=1, source_target_pairs={{3,0},{4,1},{5,2},{6,3},{7,4},{8,5},{9,6},{10,7},{11,8},{12,9},{13... | collective-permute-start | bytes 3145736 | tf_op jit(solution)/shard_map/ppermute | solution.py:26
  532.7 2.2 fusion.48
  535.0 6.0 collective-permute-done.30
  541.0 43.7 %collective-permute-start.25 = (f32[128,2048]{1,0:T(8,128)}, f32[128,2048]{1,0:T(8,128)S(1)}, u32[]{:S(2)}, u32[]{:S(2)}) collective-permute-start(f32[128,2048]{1,0:T(8,128)} %get-tuple-element.305), channel_id=1, source_target_pairs={{2,0},{3,1},{4,2},{5,3},{6,4},{7,5},{8,6},{9,7},{10,8},{11,9},{12,... | collective-permute-start | bytes 3145736 | tf_op jit(solution)/shard_map/ppermute | solution.py:26
  584.7 7.6 collective-permute-done.29
  592.3 19.6 %collective-permute-start.31 = (f32[128,2048]{1,0:T(8,128)S(1)}, f32[128,2048]{1,0:T(8,128)S(1)}, u32[]{:S(2)}, u32[]{:S(2)}) collective-permute-start(f32[128,2048]{1,0:T(8,128)S(1)} %get-tuple-element.306), channel_id=1, source_target_pairs={{8,0},{9,1},{10,2},{11,3},{12,4},{13,5},{14,6},{15,7},{16,8},{17,9... | collective-permute-start | bytes 3145736 | tf_op jit(solution)/shard_map/ppermute | solution.py:26
  611.9 26.0 %collective-permute-done.28 = f32[128,2048]{1,0:T(8,128)S(1)} collective-permute-done((f32[128,2048]{1,0:T(8,128)}, f32[128,2048]{1,0:T(8,128)S(1)}, u32[]{:S(2)}, u32[]{:S(2)}) %collective-permute-start.28) | collective-permute-done | bytes 1048608 | tf_op jit(solution)/shard_map/ppermute | solution.py:26
  637.9 5.6 collective-permute-start.16
  643.5 18.8 %collective-permute-done.27 = f32[128,2048]{1,0:T(8,128)S(1)} collective-permute-done((f32[128,2048]{1,0:T(8,128)}, f32[128,2048]{1,0:T(8,128)S(1)}, u32[]{:S(2)}, u32[]{:S(2)}) %collective-permute-start.27) | collective-permute-done | bytes 1048608 | tf_op jit(solution)/shard_map/ppermute | solution.py:26
  664.2 18.8 %collective-permute-done.26 = f32[128,2048]{1,0:T(8,128)S(1)} collective-permute-done((f32[128,2048]{1,0:T(8,128)}, f32[128,2048]{1,0:T(8,128)S(1)}, u32[]{:S(2)}, u32[]{:S(2)}) %collective-permute-start.26) | collective-permute-done | bytes 1048608 | tf_op jit(solution)/shard_map/ppermute | solution.py:26
  683.0 2.6 collective-permute-start.21
  685.7 20.4 %collective-permute-done.25 = f32[128,2048]{1,0:T(8,128)S(1)} collective-permute-done((f32[128,2048]{1,0:T(8,128)}, f32[128,2048]{1,0:T(8,128)S(1)}, u32[]{:S(2)}, u32[]{:S(2)}) %collective-permute-start.25) | collective-permute-done | bytes 1048608 | tf_op jit(solution)/shard_map/ppermute | solution.py:26
  708.0 63.2 %collective-permute-done.31 = f32[128,2048]{1,0:T(8,128)S(1)} collective-permute-done((f32[128,2048]{1,0:T(8,128)S(1)}, f32[128,2048]{1,0:T(8,128)S(1)}, u32[]{:S(2)}, u32[]{:S(2)}) %collective-permute-start.31) | collective-permute-done | bytes 1048608 | tf_op jit(solution)/shard_map/ppermute | solution.py:26
  773.1 19.2 %collective-permute-done.16 = f32[128,2048]{1,0:T(8,128)S(1)} collective-permute-done((f32[128,2048]{1,0:T(8,128)}, f32[128,2048]{1,0:T(8,128)S(1)}, u32[]{:S(2)}, u32[]{:S(2)}) %collective-permute-start.16) | collective-permute-done | bytes 1048608 | tf_op jit(solution)/shard_map/ppermute | solution.py:26
  794.3 39.8 %collective-permute-done.22 = f32[128,2048]{1,0:T(8,128)S(1)} collective-permute-done((f32[128,2048]{1,0:T(8,128)}, f32[128,2048]{1,0:T(8,128)S(1)}, u32[]{:S(2)}, u32[]{:S(2)}) %collective-permute-start.22) | collective-permute-done | bytes 1048608 | tf_op jit(solution)/shard_map/ppermute | solution.py:26
  836.0 30.5 %collective-permute-done.21 = f32[128,2048]{1,0:T(8,128)S(1)} collective-permute-done((f32[128,2048]{1,0:T(8,128)}, f32[128,2048]{1,0:T(8,128)S(1)}, u32[]{:S(2)}, u32[]{:S(2)}) %collective-permute-start.21) | collective-permute-done | bytes 1048608 | tf_op jit(solution)/shard_map/ppermute | solution.py:26
  866.5 5.3 collective-permute-start.23
  871.9 2.8 add_convert_fusion
  874.7 21.7 %collective-permute-done.20 = f32[128,2048]{1,0:T(8,128)S(1)} collective-permute-done((f32[128,2048]{1,0:T(8,128)S(1)}, f32[128,2048]{1,0:T(8,128)S(1)}, u32[]{:S(2)}, u32[]{:S(2)}) %collective-permute-start.20) | collective-permute-done | bytes 1048608 | tf_op jit(solution)/shard_map/ppermute | solution.py:26
  896.4 24.3 %collective-permute-done.19 = f32[128,2048]{1,0:T(8,128)S(1)} collective-permute-done((f32[128,2048]{1,0:T(8,128)S(1)}, f32[128,2048]{1,0:T(8,128)S(1)}, u32[]{:S(2)}, u32[]{:S(2)}) %collective-permute-start.19) | collective-permute-done | bytes 1048608 | tf_op jit(solution)/shard_map/ppermute | solution.py:26
  920.7 21.1 %collective-permute-done.18 = f32[128,2048]{1,0:T(8,128)S(1)} collective-permute-done((f32[128,2048]{1,0:T(8,128)S(1)}, f32[128,2048]{1,0:T(8,128)S(1)}, u32[]{:S(2)}, u32[]{:S(2)}) %collective-permute-start.18) | collective-permute-done | bytes 1048608 | tf_op jit(solution)/shard_map/ppermute | solution.py:26
  941.9 42.8 %collective-permute-done.17 = f32[128,2048]{1,0:T(8,128)S(1)} collective-permute-done((f32[128,2048]{1,0:T(8,128)S(1)}, f32[128,2048]{1,0:T(8,128)S(1)}, u32[]{:S(2)}, u32[]{:S(2)}) %collective-permute-start.17) | collective-permute-done | bytes 1048608 | tf_op jit(solution)/shard_map/ppermute | solution.py:26
  984.7 34.8 %collective-permute-done.23 = f32[128,2048]{1,0:T(8,128)S(1)} collective-permute-done((f32[128,2048]{1,0:T(8,128)S(1)}, f32[128,2048]{1,0:T(8,128)S(1)}, u32[]{:S(2)}, u32[]{:S(2)}) %collective-permute-start.23) | collective-permute-done | bytes 1048608 | tf_op jit(solution)/shard_map/ppermute | solution.py:26
  (281 shorter events, 213.0 us)
Async XLA Ops:
  0.6 108.8 %copy-start.3 = (bf16[128,2048]{1,0:T(8,128)(2,1)S(1)}, bf16[128,2048]{1,0:T(8,128)(2,1)}, u32[]{:S(2)}) copy-start(bf16[128,2048]{1,0:T(8,128)(2,1)} %param.15) | copy-start | bytes 1572868
  0.6 29.2 %collective-permute-start.8 = (bf16[128,2048]{1,0:T(8,128)(2,1)}, bf16[128,2048]{1,0:T(8,128)(2,1)S(1)}, u32[]{:S(2)}, u32[]{:S(2)}) collective-permute-start(bf16[128,2048]{1,0:T(8,128)(2,1)} %param.15), channel_id=1, source_target_pairs={{0,8},{1,9},{2,10},{3,11},{4,12},{5,13},{6,14},{7,15},{8,16},{9,17... | collective-permute-start | bytes 1572872 | tf_op jit(solution)/shard_map/ppermute | solution.py:26
  4.0 231.1 %collective-permute-start.7 = (bf16[128,2048]{0,1:T(8,128)(2,1)S(1)}, bf16[128,2048]{0,1:T(8,128)(2,1)S(1)}, u32[]{:S(2)}, u32[]{:S(2)}) collective-permute-start(bf16[128,2048]{0,1:T(8,128)(2,1)S(1)} %copy.31), channel_id=1, source_target_pairs={{0,1},{1,2},{2,3},{3,4},{4,5},{5,6},{6,7},{7,8},{8,9},{9,10},{10,1... | collective-permute-start | bytes 1572872 | tf_op jit(solution)/shard_map/ppermute | solution.py:26
  5.9 229.0 %collective-permute-start.6 = (bf16[128,2048]{0,1:T(8,128)(2,1)S(1)}, bf16[128,2048]{0,1:T(8,128)(2,1)S(1)}, u32[]{:S(2)}, u32[]{:S(2)}) collective-permute-start(bf16[128,2048]{0,1:T(8,128)(2,1)S(1)} %copy.31), channel_id=1, source_target_pairs={{0,2},{1,3},{2,4},{3,5},{4,6},{5,7},{6,8},{7,9},{8,10},{9,11},{10,... | collective-permute-start | bytes 1572872 | tf_op jit(solution)/shard_map/ppermute | solution.py:26
  9.4 51.0 %collective-permute-start.10 = (bf16[128,2048]{1,0:T(8,128)(2,1)}, bf16[128,2048]{1,0:T(8,128)(2,1)S(1)}, u32[]{:S(2)}, u32[]{:S(2)}) collective-permute-start(bf16[128,2048]{1,0:T(8,128)(2,1)} %param.15), channel_id=1, source_target_pairs={{0,6},{1,7},{2,8},{3,9},{4,10},{5,11},{6,12},{7,13},{8,14},{9,15},... | collective-permute-start | bytes 1572872 | tf_op jit(solution)/shard_map/ppermute | solution.py:26
  13.0 41.9 %collective-permute-start.9 = (bf16[128,2048]{1,0:T(8,128)(2,1)}, bf16[128,2048]{1,0:T(8,128)(2,1)}, u32[]{:S(2)}, u32[]{:S(2)}) collective-permute-start(bf16[128,2048]{1,0:T(8,128)(2,1)} %param.15), channel_id=1, source_target_pairs={{0,7},{1,8},{2,9},{3,10},{4,11},{5,12},{6,13},{7,14},{8,15},{9,16}... | collective-permute-start | bytes 1572872 | tf_op jit(solution)/shard_map/ppermute | solution.py:26
  29.8 77.6 %collective-permute-start.11 = (bf16[128,2048]{1,0:T(8,128)(2,1)}, bf16[128,2048]{1,0:T(8,128)(2,1)S(1)}, u32[]{:S(2)}, u32[]{:S(2)}) collective-permute-start(bf16[128,2048]{1,0:T(8,128)(2,1)} %param.15), channel_id=1, source_target_pairs={{0,5},{1,6},{2,7},{3,8},{4,9},{5,10},{6,11},{7,12},{8,13},{9,14},{... | collective-permute-start | bytes 1572872 | tf_op jit(solution)/shard_map/ppermute | solution.py:26
  54.9 54.6 %collective-permute-start.12 = (bf16[128,2048]{1,0:T(8,128)(2,1)}, bf16[128,2048]{1,0:T(8,128)(2,1)S(1)}, u32[]{:S(2)}, u32[]{:S(2)}) collective-permute-start(bf16[128,2048]{1,0:T(8,128)(2,1)} %param.15), channel_id=1, source_target_pairs={{0,4},{1,5},{2,6},{3,7},{4,8},{5,9},{6,10},{7,11},{8,12},{9,13},{1... | collective-permute-start | bytes 1572872 | tf_op jit(solution)/shard_map/ppermute | solution.py:26
  60.3 51.1 %collective-permute-start.13 = (bf16[128,2048]{1,0:T(8,128)(2,1)}, bf16[128,2048]{1,0:T(8,128)(2,1)S(1)}, u32[]{:S(2)}, u32[]{:S(2)}) collective-permute-start(bf16[128,2048]{1,0:T(8,128)(2,1)} %param.15), channel_id=1, source_target_pairs={{0,3},{1,4},{2,5},{3,6},{4,7},{5,8},{6,9},{7,10},{8,11},{9,12},{10... | collective-permute-start | bytes 1572872 | tf_op jit(solution)/shard_map/ppermute | solution.py:26
  107.5 30.3 %collective-permute-start.14 = (bf16[128,2048]{1,0:T(8,128)(2,1)}, bf16[128,2048]{1,0:T(8,128)(2,1)S(1)}, u32[]{:S(2)}, u32[]{:S(2)}) collective-permute-start(bf16[128,2048]{1,0:T(8,128)(2,1)} %param.15), channel_id=1, source_target_pairs={{0,2},{1,3},{2,4},{3,5},{4,6},{5,7},{6,8},{7,9},{8,10},{9,11},{10,... | collective-permute-start | bytes 1572872 | tf_op jit(solution)/shard_map/ppermute | solution.py:26
  109.4 55.5 %collective-permute-start.15 = (bf16[128,2048]{1,0:T(8,128)(2,1)S(1)}, bf16[128,2048]{1,0:T(8,128)(2,1)S(1)}, u32[]{:S(2)}, u32[]{:S(2)}) collective-permute-start(bf16[128,2048]{1,0:T(8,128)(2,1)S(1)} %copy-done.3), channel_id=1, source_target_pairs={{0,1},{1,2},{2,3},{3,4},{4,5},{5,6},{6,7},{7,8},{8,9},{9,10},{10,1... | collective-permute-start | bytes 1572872 | tf_op jit(solution)/shard_map/ppermute | solution.py:26
  111.4 79.9 %collective-permute-start.2 = (bf16[128,2048]{0,1:T(8,128)(2,1)S(1)}, bf16[128,2048]{0,1:T(8,128)(2,1)S(1)}, u32[]{:S(2)}, u32[]{:S(2)}) collective-permute-start(bf16[128,2048]{0,1:T(8,128)(2,1)S(1)} %copy.31), channel_id=1, source_target_pairs={{0,6},{1,7},{2,8},{3,9},{4,10},{5,11},{6,12},{7,13},{8,14},{9,15},... | collective-permute-start | bytes 1572872 | tf_op jit(solution)/shard_map/ppermute | solution.py:26
  137.7 32.2 %collective-permute-start = (bf16[128,2048]{0,1:T(8,128)(2,1)S(1)}, bf16[128,2048]{0,1:T(8,128)(2,1)S(1)}, u32[]{:S(2)}, u32[]{:S(2)}) collective-permute-start(bf16[128,2048]{0,1:T(8,128)(2,1)S(1)} %copy.31), channel_id=1, source_target_pairs={{0,8},{1,9},{2,10},{3,11},{4,12},{5,13},{6,14},{7,15},{8,16},{9,17... | collective-permute-start | bytes 1572872 | tf_op jit(solution)/shard_map/ppermute | solution.py:26
  164.9 22.7 %collective-permute-start.1 = (bf16[128,2048]{0,1:T(8,128)(2,1)S(1)}, bf16[128,2048]{0,1:T(8,128)(2,1)S(1)}, u32[]{:S(2)}, u32[]{:S(2)}) collective-permute-start(bf16[128,2048]{0,1:T(8,128)(2,1)S(1)} %copy.31), channel_id=1, source_target_pairs={{0,7},{1,8},{2,9},{3,10},{4,11},{5,12},{6,13},{7,14},{8,15},{9,16}... | collective-permute-start | bytes 1572872 | tf_op jit(solution)/shard_map/ppermute | solution.py:26
  166.9 68.3 %copy-start.2 = (bf16[1152,2048]{1,0:T(8,128)(2,1)}, bf16[1152,2048]{1,0:T(8,128)(2,1)S(1)}, u32[]{:S(2)}) copy-start(bf16[1152,2048]{1,0:T(8,128)(2,1)S(1)} %constant_dynamic-update-slice_fusion.11) | copy-start | bytes 14155780
  169.9 58.3 %collective-permute-start.3 = (bf16[128,2048]{0,1:T(8,128)(2,1)S(1)}, bf16[128,2048]{0,1:T(8,128)(2,1)S(1)}, u32[]{:S(2)}, u32[]{:S(2)}) collective-permute-start(bf16[128,2048]{0,1:T(8,128)(2,1)S(1)} %copy.31), channel_id=1, source_target_pairs={{0,5},{1,6},{2,7},{3,8},{4,9},{5,10},{6,11},{7,12},{8,13},{9,14},{... | collective-permute-start | bytes 1572872 | tf_op jit(solution)/shard_map/ppermute | solution.py:26
  187.6 40.8 %collective-permute-start.4 = (bf16[128,2048]{0,1:T(8,128)(2,1)S(1)}, bf16[128,2048]{0,1:T(8,128)(2,1)S(1)}, u32[]{:S(2)}, u32[]{:S(2)}) collective-permute-start(bf16[128,2048]{0,1:T(8,128)(2,1)S(1)} %copy.31), channel_id=1, source_target_pairs={{0,4},{1,5},{2,6},{3,7},{4,8},{5,9},{6,10},{7,11},{8,12},{9,13},{1... | collective-permute-start | bytes 1572872 | tf_op jit(solution)/shard_map/ppermute | solution.py:26
  191.4 43.4 %collective-permute-start.5 = (bf16[128,2048]{0,1:T(8,128)(2,1)S(1)}, bf16[128,2048]{0,1:T(8,128)(2,1)S(1)}, u32[]{:S(2)}, u32[]{:S(2)}) collective-permute-start(bf16[128,2048]{0,1:T(8,128)(2,1)S(1)} %copy.31), channel_id=1, source_target_pairs={{0,3},{1,4},{2,5},{3,6},{4,7},{5,8},{6,9},{7,10},{8,11},{9,12},{10... | collective-permute-start | bytes 1572872 | tf_op jit(solution)/shard_map/ppermute | solution.py:26
  235.4 2.2 copy-start.4
  473.5 7.1 copy-start.1
  473.5 59.2 %copy-start = (f32[1152,2048]{1,0:T(8,128)S(1)}, f32[1152,2048]{1,0:T(8,128)}, u32[]{:S(2)}) copy-start(f32[1152,2048]{1,0:T(8,128)} %get-tuple-element.218) | copy-start | bytes 28311556
  480.6 38.8 %collective-permute-start.24 = (f32[128,2048]{1,0:T(8,128)S(1)}, f32[128,2048]{1,0:T(8,128)S(1)}, u32[]{:S(2)}, u32[]{:S(2)}) collective-permute-start(f32[128,2048]{1,0:T(8,128)S(1)} %get-tuple-element.299), channel_id=1, source_target_pairs={{1,0},{2,1},{3,2},{4,3},{5,4},{6,5},{7,6},{8,7},{9,8},{10,9},{11,1... | collective-permute-start | bytes 3145736 | tf_op jit(solution)/shard_map/ppermute | solution.py:26
  500.5 40.5 %collective-permute-start.30 = (f32[128,2048]{1,0:T(8,128)}, f32[128,2048]{1,0:T(8,128)S(1)}, u32[]{:S(2)}, u32[]{:S(2)}) collective-permute-start(f32[128,2048]{1,0:T(8,128)} %get-tuple-element.300), channel_id=1, source_target_pairs={{7,0},{8,1},{9,2},{10,3},{11,4},{12,5},{13,6},{14,7},{15,8},{16,9}... | collective-permute-start | bytes 3145736 | tf_op jit(solution)/shard_map/ppermute | solution.py:26
  502.5 89.8 %collective-permute-start.29 = (f32[128,2048]{1,0:T(8,128)}, f32[128,2048]{1,0:T(8,128)S(1)}, u32[]{:S(2)}, u32[]{:S(2)}) collective-permute-start(f32[128,2048]{1,0:T(8,128)} %get-tuple-element.301), channel_id=1, source_target_pairs={{6,0},{7,1},{8,2},{9,3},{10,4},{11,5},{12,6},{13,7},{14,8},{15,9},... | collective-permute-start | bytes 3145736 | tf_op jit(solution)/shard_map/ppermute | solution.py:26
  512.4 125.5 %collective-permute-start.28 = (f32[128,2048]{1,0:T(8,128)}, f32[128,2048]{1,0:T(8,128)S(1)}, u32[]{:S(2)}, u32[]{:S(2)}) collective-permute-start(f32[128,2048]{1,0:T(8,128)} %get-tuple-element.302), channel_id=1, source_target_pairs={{5,0},{6,1},{7,2},{8,3},{9,4},{10,5},{11,6},{12,7},{13,8},{14,9},{... | collective-permute-start | bytes 3145736 | tf_op jit(solution)/shard_map/ppermute | solution.py:26
  517.5 144.8 %collective-permute-start.27 = (f32[128,2048]{1,0:T(8,128)}, f32[128,2048]{1,0:T(8,128)S(1)}, u32[]{:S(2)}, u32[]{:S(2)}) collective-permute-start(f32[128,2048]{1,0:T(8,128)} %get-tuple-element.303), channel_id=1, source_target_pairs={{4,0},{5,1},{6,2},{7,3},{8,4},{9,5},{10,6},{11,7},{12,8},{13,9},{1... | collective-permute-start | bytes 3145736 | tf_op jit(solution)/shard_map/ppermute | solution.py:26
  519.4 163.6 %collective-permute-start.26 = (f32[128,2048]{1,0:T(8,128)}, f32[128,2048]{1,0:T(8,128)S(1)}, u32[]{:S(2)}, u32[]{:S(2)}) collective-permute-start(f32[128,2048]{1,0:T(8,128)} %get-tuple-element.304), channel_id=1, source_target_pairs={{3,0},{4,1},{5,2},{6,3},{7,4},{8,5},{9,6},{10,7},{11,8},{12,9},{13... | collective-permute-start | bytes 3145736 | tf_op jit(solution)/shard_map/ppermute | solution.py:26
  541.0 165.1 %collective-permute-start.25 = (f32[128,2048]{1,0:T(8,128)}, f32[128,2048]{1,0:T(8,128)S(1)}, u32[]{:S(2)}, u32[]{:S(2)}) collective-permute-start(f32[128,2048]{1,0:T(8,128)} %get-tuple-element.305), channel_id=1, source_target_pairs={{2,0},{3,1},{4,2},{5,3},{6,4},{7,5},{8,6},{9,7},{10,8},{11,9},{12,... | collective-permute-start | bytes 3145736 | tf_op jit(solution)/shard_map/ppermute | solution.py:26
  592.3 178.9 %collective-permute-start.31 = (f32[128,2048]{1,0:T(8,128)S(1)}, f32[128,2048]{1,0:T(8,128)S(1)}, u32[]{:S(2)}, u32[]{:S(2)}) collective-permute-start(f32[128,2048]{1,0:T(8,128)S(1)} %get-tuple-element.306), channel_id=1, source_target_pairs={{8,0},{9,1},{10,2},{11,3},{12,4},{13,5},{14,6},{15,7},{16,8},{17,9... | collective-permute-start | bytes 3145736 | tf_op jit(solution)/shard_map/ppermute | solution.py:26
  637.9 154.4 %collective-permute-start.16 = (f32[128,2048]{1,0:T(8,128)}, f32[128,2048]{1,0:T(8,128)S(1)}, u32[]{:S(2)}, u32[]{:S(2)}) collective-permute-start(f32[128,2048]{1,0:T(8,128)} %get-tuple-element.307), channel_id=1, source_target_pairs={{1,0},{2,1},{3,2},{4,3},{5,4},{6,5},{7,6},{8,7},{9,8},{10,9},{11,1... | collective-permute-start | bytes 3145736 | tf_op jit(solution)/shard_map/ppermute | solution.py:26
  662.3 171.8 %collective-permute-start.22 = (f32[128,2048]{1,0:T(8,128)}, f32[128,2048]{1,0:T(8,128)S(1)}, u32[]{:S(2)}, u32[]{:S(2)}) collective-permute-start(f32[128,2048]{1,0:T(8,128)} %get-tuple-element.308), channel_id=1, source_target_pairs={{7,0},{8,1},{9,2},{10,3},{11,4},{12,5},{13,6},{14,7},{15,8},{16,9}... | collective-permute-start | bytes 3145736 | tf_op jit(solution)/shard_map/ppermute | solution.py:26
  683.0 183.5 %collective-permute-start.21 = (f32[128,2048]{1,0:T(8,128)}, f32[128,2048]{1,0:T(8,128)S(1)}, u32[]{:S(2)}, u32[]{:S(2)}) collective-permute-start(f32[128,2048]{1,0:T(8,128)} %get-tuple-element.309), channel_id=1, source_target_pairs={{6,0},{7,1},{8,2},{9,3},{10,4},{11,5},{12,6},{13,7},{14,8},{15,9},... | collective-permute-start | bytes 3145736 | tf_op jit(solution)/shard_map/ppermute | solution.py:26
  706.1 190.3 %collective-permute-start.20 = (f32[128,2048]{1,0:T(8,128)S(1)}, f32[128,2048]{1,0:T(8,128)S(1)}, u32[]{:S(2)}, u32[]{:S(2)}) collective-permute-start(f32[128,2048]{1,0:T(8,128)S(1)} %get-tuple-element.310), channel_id=1, source_target_pairs={{5,0},{6,1},{7,2},{8,3},{9,4},{10,5},{11,6},{12,7},{13,8},{14,9},{... | collective-permute-start | bytes 3145736 | tf_op jit(solution)/shard_map/ppermute | solution.py:26
  771.2 149.5 %collective-permute-start.19 = (f32[128,2048]{1,0:T(8,128)S(1)}, f32[128,2048]{1,0:T(8,128)S(1)}, u32[]{:S(2)}, u32[]{:S(2)}) collective-permute-start(f32[128,2048]{1,0:T(8,128)S(1)} %get-tuple-element.311), channel_id=1, source_target_pairs={{4,0},{5,1},{6,2},{7,3},{8,4},{9,5},{10,6},{11,7},{12,8},{13,9},{1... | collective-permute-start | bytes 3145736 | tf_op jit(solution)/shard_map/ppermute | solution.py:26
  792.3 149.5 %collective-permute-start.18 = (f32[128,2048]{1,0:T(8,128)S(1)}, f32[128,2048]{1,0:T(8,128)S(1)}, u32[]{:S(2)}, u32[]{:S(2)}) collective-permute-start(f32[128,2048]{1,0:T(8,128)S(1)} %get-tuple-element.312), channel_id=1, source_target_pairs={{3,0},{4,1},{5,2},{6,3},{7,4},{8,5},{9,6},{10,7},{11,8},{12,9},{13... | collective-permute-start | bytes 3145736 | tf_op jit(solution)/shard_map/ppermute | solution.py:26
  834.1 150.6 %collective-permute-start.17 = (f32[128,2048]{1,0:T(8,128)S(1)}, f32[128,2048]{1,0:T(8,128)S(1)}, u32[]{:S(2)}, u32[]{:S(2)}) collective-permute-start(f32[128,2048]{1,0:T(8,128)S(1)} %get-tuple-element.313), channel_id=1, source_target_pairs={{2,0},{3,1},{4,2},{5,3},{6,4},{7,5},{8,6},{9,7},{10,8},{11,9},{12,... | collective-permute-start | bytes 3145736 | tf_op jit(solution)/shard_map/ppermute | solution.py:26
  866.5 153.0 %collective-permute-start.23 = (f32[128,2048]{1,0:T(8,128)S(1)}, f32[128,2048]{1,0:T(8,128)S(1)}, u32[]{:S(2)}, u32[]{:S(2)}) collective-permute-start(f32[128,2048]{1,0:T(8,128)S(1)} %get-tuple-element.314), channel_id=1, source_target_pairs={{8,0},{9,1},{10,2},{11,3},{12,4},{13,5},{14,6},{15,7},{16,8},{17,9... | collective-permute-start | bytes 3145736 | tf_op jit(solution)/shard_map/ppermute | solution.py:26
where the time goes:
time: 1030 us; the launch traced here: 1020 us
  waiting for transfers between devices  481 us (47%)
  starting transfers between devices  283 us (27%)
  matrix products  163 us (16%)
  local copies, waits for them, and re-layouts  70.6 us (7%)
  other arithmetic  21 us (2%)
    ppermute x32, waiting for transfers between devices, passed_along(): lax.ppermute(value, axis, [(source, source + steps) for source in range(f...  481 us
    ppermute x32, starting transfers between devices, passed_along(): lax.ppermute(value, axis, [(source, source + steps) for source in range(f...  283 us
    dot_general x16, matrix products, one_head(): jnp.einsum('hrk,rhd->kd', weights_low, o_head, preferred_element_type=jnp...  45 us
    dot_general x16, matrix products, one_head(): jnp.einsum('hrk,kd->rhd', weights_low, v_head, preferred_element_type=jnp...  31.1 us
    sub x16, matrix products, one_head(): exponent = jnp.exp(scores - row_max)  25.1 us
    dot_general x16, matrix products, one_head(): jnp.einsum('rhd,kd->hrk', o_head, v_head, preferred_element_type=jnp.floa...  22.7 us
  transfers between devices with their start and end apart: 32, of which 23 were waited for; matrix products, arithmetic and copies ran while one was open for 1% of the time, Pallas kernels for 0%

commit v1 on v0

v1 whole, which is shorter than its diff:
```python
import math

import jax
import jax.numpy as jnp
from jax import lax
from jax.experimental import pallas as pl
from jax.experimental.pallas import tpu as pltpu
from jax.sharding import PartitionSpec as P


HEAD_DIM = 128
WINDOW = 1024
MESH = pl.DeviceIdType.MESH
NEG = -1e30
BIG = 1e30
SCALE = 168.0 ** (-0.5)
SCALE2 = SCALE * math.log2(math.e)
F32 = jnp.float32
BF16 = jnp.bfloat16
ROWS = 128
PEERS = 4
HEADS = 4
OWN = PEERS * ROWS
SPAN = WINDOW + OWN
KEYS = WINDOW + ROWS
BLOCKS = KEYS // ROWS


def kernel(
    n_seq,
    q_ref,
    k_ref,
    v_ref,
    g_ref,
    o_out,
    dq_out,
    dk_out,
    dv_out,
    kv,
    qd,
    od,
    grad,
    first_stage,
    second_stage,
    last_stage,
    got_first,
    got_second,
    k_t,
    v_t,
    scores,
    probs,
    dscores,
    kv_in,
    qd_in,
    in_send,
    halo_recv,
    halo_send,
    grad_recv,
    grad_send,
    out_recv,
    out_send,
):
    seq = lax.axis_index("seq")
    kvh = lax.axis_index("kvh")
    half = n_seq // 2

    def slot_of(group, position):
        return lax.rem(position + 2 * lax.div(group, half), PEERS)

    slot = slot_of(seq, kvh)
    has_prev = seq > 0
    has_next = seq < n_seq - 1
    prev = (seq - 1, slot_of(seq - 1, slot))
    next_ = (seq + 1, slot_of(seq + 1, slot))

    def await_bytes(ref, sem):
        pltpu.make_async_copy(ref, ref, sem).wait()

    barrier = pltpu.get_barrier_semaphore()
    for step in range(1, PEERS):
        pl.semaphore_signal(
            barrier, inc=1, device_id=(seq, lax.rem(kvh + step, PEERS)), device_id_type=MESH
        )

    @pl.when(has_prev)
    def _():
        pl.semaphore_signal(barrier, inc=1, device_id=prev, device_id_type=MESH)

    @pl.when(has_next)
    def _():
        pl.semaphore_signal(barrier, inc=1, device_id=next_, device_id_type=MESH)

    neighbours = has_prev.astype(jnp.int32) + has_next.astype(jnp.int32)
    pl.semaphore_wait(barrier, PEERS - 1 + neighbours)

    my_rows = pl.ds(pl.multiple_of(WINDOW + kvh * ROWS, ROWS), ROWS)
    my_own = pl.ds(pl.multiple_of(kvh * ROWS, ROWS), ROWS)

    def send_inputs(head, carry):
        for array, (source, wide, buffer) in enumerate(
            ((k_ref, 1, kv), (v_ref, 1, kv), (q_ref, 2, qd), (g_ref, 2, qd))
        ):
            width = wide * HEAD_DIM
            for step in range(PEERS):
                position = lax.rem(kvh + step, PEERS)
                column = (slot_of(seq, position) * HEADS + head) * width
                src = source.at[:, pl.ds(pl.multiple_of(column, HEAD_DIM), width)]
                dst = buffer.at[head, array % 2, my_rows if wide == 1 else my_own, :]
                sem = kv_in.at[head] if wide == 1 else qd_in.at[head]
                if step == 0:
                    pltpu.make_async_copy(src, dst, sem).start()
                else:
                    pltpu.make_async_remote_copy(
                        src_ref=src,
                        dst_ref=dst,
                        send_sem=in_send.at[array],
                        recv_sem=sem,
                        device_id=(seq, position),
                        device_id_type=MESH,
                    ).start()
        return carry

    lax.fori_loop(0, HEADS, send_inputs, 0)

    @pl.when(jnp.logical_not(has_prev))
    def _():
        for head in range(HEADS):
            kv[head, :, pl.ds(0, WINDOW), :] = jnp.zeros((2, WINDOW, HEAD_DIM), BF16)

    @pl.when(jnp.logical_not(has_next))
    def _():
        got_first[...] = jnp.zeros(got_first.shape, BF16)
        got_second[...] = jnp.zeros(got_second.shape, BF16)

    def halo(head, hop):
        return pltpu.make_async_remote_copy(
            src_ref=kv.at[head, :, pl.ds(WINDOW - hop * OWN, OWN), :],
            dst_ref=kv.at[head, :, pl.ds(WINDOW - (hop + 1) * OWN, OWN), :],
            send_sem=halo_send.at[hop, head],
            recv_sem=halo_recv.at[hop, head],
            device_id=next_,
            device_id_type=MESH,
        )

    def send_own(head):
        await_bytes(kv.at[head, :, pl.ds(WINDOW, OWN), :], kv_in.at[head])

        @pl.when(has_next)
        def _():
            halo(head, 0).start()

    def pass_on(head):
        @pl.when(has_prev)
        def _():
            await_bytes(kv.at[head, :, pl.ds(OWN, OWN), :], halo_recv.at[0, head])

        @pl.when(has_next)
        def _():
            halo(head, 1).start()

    def await_halo(head):
        @pl.when(has_prev)
        def _():
            await_bytes(kv.at[head, :, pl.ds(0, OWN), :], halo_recv.at[1, head])

    def grad_copy(stage, buffer, hop, head):
        return pltpu.make_async_remote_copy(
            src_ref=stage.at[head],
            dst_ref=buffer.at[head],
            send_sem=grad_send.at[hop, head],
            recv_sem=grad_recv.at[hop, head],
            device_id=prev,
            device_id_type=MESH,
        )

    def grads_first(head):
        for half_ in range(2):
            first_stage[head, half_] = grad[head, half_, pl.ds(0, OWN), :].astype(BF16)

        @pl.when(has_prev)
        def _():
            grad_copy(first_stage, got_first, 0, head).start()

    def grads_second(head):
        @pl.when(has_next)
        def _():
            await_bytes(got_first.at[head], grad_recv.at[0, head])

        for half_ in range(2):
            second_stage[head, half_] = (
                grad[head, half_, pl.ds(OWN, OWN), :] + got_first[head, half_].astype(F32)
            ).astype(BF16)

        @pl.when(has_prev)
        def _():
            grad_copy(second_stage, got_second, 1, head).start()

    def send_back(source, wide, out, array, head):
        width = wide * HEAD_DIM
        column = pl.multiple_of((slot * HEADS + head) * width, HEAD_DIM)
        for step in range(PEERS):
            position = lax.rem(kvh + step, PEERS)
            src = source.at[pl.ds(pl.multiple_of(position * ROWS, ROWS), ROWS), :]
            dst = out.at[:, pl.ds(column, width)]
            if step == 0:
                pltpu.make_async_copy(src, dst, out_recv.at[array]).start()
            else:
                pltpu.make_async_remote_copy(
                    src_ref=src,
                    dst_ref=dst,
                    send_sem=out_send.at[array],
                    recv_sem=out_recv.at[array],
                    device_id=(seq, position),
                    device_id_type=MESH,
                ).start()

    def grads_last(head):
        @pl.when(has_next)
        def _():
            await_bytes(got_second.at[head], grad_recv.at[1, head])

        for half_ in range(2):
            last_stage[head, half_] = (
                grad[head, half_, pl.ds(WINDOW, OWN), :] + got_second[head, half_].astype(F32)
            ).astype(BF16)
        send_back(last_stage.at[head, 0], 1, dk_out, 2, head)
        send_back(last_stage.at[head, 1], 1, dv_out, 3, head)

    low = jnp.where(seq == 0, WINDOW // ROWS, jnp.where(seq == 1, (WINDOW - OWN) // ROWS, 0))
    key_at = lax.broadcasted_iota(jnp.int32, (ROWS, 2 * ROWS), 0)
    row_at = lax.rem(lax.broadcasted_iota(jnp.int32, (ROWS, 2 * ROWS), 1), ROWS)

    def turned(block):
        block = block.astype(F32)
        return jnp.concatenate(
            [block[:, :HEAD_DIM].T, block[:, HEAD_DIM:].T], axis=1
        )

    def dot(a, b):
        return jnp.dot(a, b, preferred_element_type=F32)

    def dot_t(a, b):
        return lax.dot_general(a, b, (((1,), (1,)), ((), ())), preferred_element_type=F32)

    def transposed_keys(head):
        for piece in range(SPAN // ROWS):
            rows = pl.ds(piece * ROWS, ROWS)
            k_t[:, rows] = kv[head, 0, rows, :].astype(F32).T.astype(BF16)
            v_t[:, rows] = kv[head, 1, rows, :].astype(F32).T.astype(BF16)

    def query_block(head, block):
        start = pl.multiple_of(block * ROWS, ROWS)
        rows = pl.ds(start, ROWS)
        q_t = turned(qd[head, 0, rows, :])
        g_t = turned(qd[head, 1, rows, :])
        q_low = q_t.astype(BF16)
        g_low = g_t.astype(BF16)
        top = None
        for piece in range(BLOCKS):
            keys = kv[head, 0, pl.ds(start + piece * ROWS, ROWS), :]
            s = dot(keys, q_low)
            if piece == 0:
                s = jnp.where(key_at > row_at, s, NEG)
            if piece == BLOCKS - 1:
                s = jnp.where(key_at <= row_at, s, NEG)
            scores[pl.ds(piece * ROWS, ROWS), :] = s
            best = s.reshape(ROWS // 8, 8, 2 * ROWS).max(axis=0)
            if piece < BLOCKS - 1:
                best = jnp.where(block + piece >= low, best, NEG)
            top = best if top is None else jnp.maximum(top, best)
        top = top.max(axis=0, keepdims=True) * SCALE2
        total = jnp.zeros((8, 2 * ROWS), F32)
        for piece in range(BLOCKS):
            here = pl.ds(piece * ROWS, ROWS)
            shift = top
            if piece < BLOCKS - 1:
                shift = jnp.where(block + piece >= low, top, BIG)
            p = jnp.exp2(scores[here, :] * SCALE2 - shift)
            total = total + p.reshape(ROWS // 8, 8, 2 * ROWS).sum(axis=0)
            probs[here, :] = p.astype(BF16)
        inverse = 1.0 / total.sum(axis=0, keepdims=True)
        window = pl.ds(start, KEYS)
        o_t = dot(v_t[:, window], probs[...]) * inverse
        delta = (o_t * g_t).sum(axis=0, keepdims=True)
        q_scaled = (q_t * (inverse * SCALE)).astype(BF16)
        g_scaled = (g_t * inverse).astype(BF16)
        for piece in range(BLOCKS):
            here = pl.ds(piece * ROWS, ROWS)
            there = pl.ds(start + piece * ROWS, ROWS)
            dp = dot(kv[head, 1, there, :], g_low)
            p = probs[here, :]
            ds = (p.astype(F32) * (dp - delta)).astype(BF16)
            dscores[here, :] = ds
            dv = dot_t(p, g_scaled)
            dk = dot_t(ds, q_scaled)
            if piece < BLOCKS - 1:
                grad[head, 1, there, :] += dv
                grad[head, 0, there, :] += dk
            else:
                grad[head, 1, there, :] = dv
                grad[head, 0, there, :] = dk
        dq_t = dot(k_t[:, window], dscores[...]) * (inverse * SCALE)
        for index, value in enumerate((o_t, dq_t)):
            for side in range(2):
                cols = slice(side * ROWS, (side + 1) * ROWS)
                od[head, index, rows, cols] = value[:, cols].T.astype(BF16)

    send_own(0)
    pass_on(0)
    send_own(1)

    def one_head(head, carry):
        await_bytes(qd.at[head], qd_in.at[head])
        await_halo(head)
        grad[head, :, pl.ds(0, WINDOW), :] = jnp.zeros((2, WINDOW, HEAD_DIM), F32)
        transposed_keys(head)

        def one_block(block, carry):
            query_block(head, block)

            @pl.when((block == 1) & (head < HEADS - 1))
            def _():
                pass_on(head + 1)

            @pl.when((block == 1) & (head < HEADS - 2))
            def _():
                send_own(head + 2)

            @pl.when((block == 2) & (head > 0))
            def _():
                grads_second(head - 1)

            return carry

        lax.fori_loop(0, PEERS, one_block, 0)
        grads_first(head)
        send_back(od.at[head, 0], 2, o_out, 0, head)
        send_back(od.at[head, 1], 2, dq_out, 1, head)

        @pl.when(head > 0)
        def _():
            grads_last(head - 1)

        return carry

    lax.fori_loop(0, HEADS, one_head, 0)
    grads_second(HEADS - 1)
    grads_last(HEADS - 1)

    for array, buffer in enumerate((kv, kv, qd, qd)):
        region = pl.ds(0, OWN)
        await_bytes(buffer.at[pl.ds(0, PEERS - 1), 0, region, :], in_send.at[array])
    for hop in range(2):
        for head in range(HEADS):

            @pl.when(has_next)
            def _():
                halo(head, hop).wait_send()

            @pl.when(has_prev)
            def _():
                stage, buffer = ((first_stage, got_first), (second_stage, got_second))[hop]
                grad_copy(stage, buffer, hop, head).wait_send()

    for array, (out, stage) in enumerate(
        (
            (o_out, od.at[pl.ds(0, PEERS - 1), 0]),
            (dq_out, od.at[pl.ds(0, PEERS - 1), 1]),
            (dk_out, last_stage.at[pl.ds(0, PEERS - 1), 0]),
            (dv_out, last_stage.at[pl.ds(0, PEERS - 1), 1]),
        )
    ):
        await_bytes(stage, out_send.at[array])
        await_bytes(out, out_recv.at[array])


def solution(mesh):
    n_seq = mesh.shape["seq"]

    def step(queries, key_rows, value_rows, grad_out):
        def call(*refs):
            kernel(n_seq, *refs)

        flops = 5 * 2 * 256 * KEYS * HEAD_DIM * HEADS * PEERS
        return pl.pallas_call(
            call,
            name="window_attention",
            out_shape=(
                jax.ShapeDtypeStruct(queries.shape, BF16),
                jax.ShapeDtypeStruct(queries.shape, BF16),
                jax.ShapeDtypeStruct(key_rows.shape, BF16),
                jax.ShapeDtypeStruct(key_rows.shape, BF16),
            ),
            in_specs=[pl.BlockSpec(memory_space=pl.ANY)] * 4,
            out_specs=[pl.BlockSpec(memory_space=pl.ANY)] * 4,
            scratch_shapes=[
                pltpu.VMEM((HEADS, 2, SPAN, HEAD_DIM), BF16),
                pltpu.VMEM((HEADS, 2, OWN, 2 * HEAD_DIM), BF16),
                pltpu.VMEM((HEADS, 2, OWN, 2 * HEAD_DIM), BF16),
                pltpu.VMEM((HEADS, 2, SPAN, HEAD_DIM), F32),
                pltpu.VMEM((HEADS, 2, OWN, HEAD_DIM), BF16),
                pltpu.VMEM((HEADS, 2, OWN, HEAD_DIM), BF16),
                pltpu.VMEM((HEADS, 2, OWN, HEAD_DIM), BF16),
                pltpu.VMEM((HEADS, 2, OWN, HEAD_DIM), BF16),
                pltpu.VMEM((HEADS, 2, OWN, HEAD_DIM), BF16),
                pltpu.VMEM((HEAD_DIM, SPAN), BF16),
                pltpu.VMEM((HEAD_DIM, SPAN), BF16),
                pltpu.VMEM((KEYS, 2 * ROWS), F32),
                pltpu.VMEM((KEYS, 2 * ROWS), BF16),
                pltpu.VMEM((KEYS, 2 * ROWS), BF16),
                pltpu.SemaphoreType.DMA((HEADS,)),
                pltpu.SemaphoreType.DMA((HEADS,)),
                pltpu.SemaphoreType.DMA((4,)),
                pltpu.SemaphoreType.DMA((2, HEADS)),
                pltpu.SemaphoreType.DMA((2, HEADS)),
                pltpu.SemaphoreType.DMA((2, HEADS)),
                pltpu.SemaphoreType.DMA((2, HEADS)),
                pltpu.SemaphoreType.DMA((4,)),
                pltpu.SemaphoreType.DMA((4,)),
            ],
            compiler_params=pltpu.CompilerParams(
                collective_id=0, has_side_effects=True, vmem_limit_bytes=60 * 1024 * 1024
            ),
            cost_estimate=pl.CostEstimate(
                flops=flops, bytes_accessed=12 * 1024 * 1024, transcendentals=0
            ),
        )(queries, key_rows, value_rows, grad_out)

    spec = P(("seq", "kvh"), None)
    return jax.shard_map(
        step, mesh=mesh, in_specs=(spec,) * 4, out_specs=(spec,) * 4, check_vma=False
    )
```

time: 1030 us -> 105 us (0.10)
  waiting for transfers between devices: 481 us -> 0 us
  starting transfers between devices: 283 us -> 0 us
  matrix products: 163 us -> 0 us
  Pallas kernels: 0 us -> 97.6 us
  local copies, waits for them, and re-layouts: 70.6 us -> 5.8 us
  other arithmetic: 21 us -> 0 us
    ppermute x32 -> x0, waiting for transfers between devices: 481 us -> none  [passed_along(): lax.ppermute(value, axis, [(source, source + steps) for source in range(f...]
    ppermute x32 -> x0, starting transfers between devices: 283 us -> none  [passed_along(): lax.ppermute(value, axis, [(source, source + steps) for source in range(f...]
    dot_general x80 -> x0, matrix products: 138 us -> none  [the longest x16 45 us: one_head(): jnp.einsum('hrk,rhd->kd', weights_low, o_head, preferred_element_type=jnp...]
    pallas_call x0 -> x1, Pallas kernels: none -> 97.6 us  [step(): pl.pallas_call(call, name='window_attention', out_shape=(jax.ShapeDtypeSt...]
    dynamic_slice x64 -> x0, local copies, waits for them, and re-layouts: 30.7 us -> none  [the longest x32 15.4 us: one_head(): lax.dynamic_slice_in_dim(queries, q_cols, 2 * HEAD_DIM, 1)]
    sub x16 -> x0, matrix products: 25.1 us -> none  [one_head(): exponent = jnp.exp(scores - row_max)]
    and x16 -> x0, other arithmetic: 13.9 us -> none  [head_loop(): (key_pos[None, :] <= query_pos[:, None]) & (query_pos[:, None] - key_pos[...]
    dynamic_update_slice x48 -> x0, local copies, waits for them, and re-layouts: 13.8 us -> none  [the longest x32 12.1 us: one_head(): lax.dynamic_update_slice_in_dim(grad_q, dq_head.reshape(row_count, 2 * HE...]
  transfers between devices with their start and end apart: 32 -> 0, of which waited for: 23 -> 0; matrix products, arithmetic and copies ran while one was open for 1% -> 0% of each run, Pallas kernels for 0% -> 0%
where the time goes in v1:
time: 105 us; the launch traced here: 104 us
  Pallas kernels  97.6 us (93%)
  local copies, waits for them, and re-layouts  5.8 us (6%)
    pallas_call x1, Pallas kernels, step(): pl.pallas_call(call, name='window_attention', out_shape=(jax.ShapeDtypeSt...  97.6 us
    unnamed x10, local copies, waits for them, and re-layouts  5.8 us

profile of v1, /device:TPU:216, one launch (start us, length us, event | category | flops | bytes accessed | tf_op | source)
XLA Modules:
  0.0 104.0 jit_solution(9536700276842237109)
XLA Ops:
  0.6 97.6 %window_attention.1 = (bf16[128,4096]{1,0:T(8,128)(2,1)}, bf16[128,4096]{1,0:T(8,128)(2,1)}, bf16[128,2048]{1,0:T(8,128)(2,1)}, bf16[128,2048]{1,0:T(8,128)(2,1)}) custom-call(bf16[128,4096]{1,0:T(8,128)(2,1)} %refs_0_.1, bf16[128,2048]{1,0:T(8,128)(2,1)} %refs_1_.1, bf16[128,2048]{1,0:T(8,128)(2,1)} %refs_2_.1, bf16[128,4096]{1,0:T(8,128)(2,1)} %refs_3_.1), custom_call_target="tpu_custom_call" | custom-call | flops 6039797760 | bytes 12582912 | tf_op jit(solution)/shard_map/window_attention/pallas_call | solution.py:385
  98.2 0.0 copy-start
  98.2 2.4 %copy.12 = bf16[128,4096]{1,0:T(8,128)(2,1)} copy(bf16[128,4096]{1,0:T(8,128)(2,1)} %get-tuple-element.8) | data formatting | bytes 2097152
  100.6 0.0 copy-done
  100.6 0.0 copy-start.2
  100.6 1.0 copy.13
  101.6 0.4 copy-done.2
  102.0 0.0 copy-start.1
  102.0 0.8 copy.14
  102.8 0.4 copy-done.1
  103.3 0.8 copy.15
Async XLA Ops:
  98.2 2.4 %copy-start = (bf16[128,4096]{1,0:T(8,128)(2,1)S(1)}, bf16[128,4096]{1,0:T(8,128)(2,1)}, u32[]{:S(2)}) copy-start(bf16[128,4096]{1,0:T(8,128)(2,1)} %get-tuple-element.9) | copy-start | bytes 3145732
  100.6 1.4 %copy-start.2 = (bf16[128,2048]{1,0:T(8,128)(2,1)S(1)}, bf16[128,2048]{1,0:T(8,128)(2,1)}, u32[]{:S(2)}) copy-start(bf16[128,2048]{1,0:T(8,128)(2,1)} %get-tuple-element.10) | copy-start | bytes 1572868
  102.0 1.2 %copy-start.1 = (bf16[128,2048]{1,0:T(8,128)(2,1)S(1)}, bf16[128,2048]{1,0:T(8,128)(2,1)}, u32[]{:S(2)}) copy-start(bf16[128,2048]{1,0:T(8,128)(2,1)} %get-tuple-element.11) | copy-start | bytes 1572868

commit v2 on v1

--- a/solution.py
+++ b/solution.py
@@ -173,13 +173,21 @@
             device_id_type=MESH,
         )
 
-    def grads_first(head):
+    def grads_first(head, block):
+        rows = pl.ds(pl.multiple_of(block * ROWS, ROWS), ROWS)
         for half_ in range(2):
-            first_stage[head, half_] = grad[head, half_, pl.ds(0, OWN), :].astype(BF16)
+            first_stage[head, half_, rows, :] = grad[head, half_, rows, :].astype(BF16)
 
         @pl.when(has_prev)
         def _():
-            grad_copy(first_stage, got_first, 0, head).start()
+            pltpu.make_async_remote_copy(
+                src_ref=first_stage.at[head, :, rows, :],
+                dst_ref=got_first.at[head, :, rows, :],
+                send_sem=grad_send.at[0, head],
+                recv_sem=grad_recv.at[0, head],
+                device_id=prev,
+                device_id_type=MESH,
+            ).start()
 
     def grads_second(head):
         @pl.when(has_next)
@@ -317,6 +325,11 @@
 
         def one_block(block, carry):
             query_block(head, block)
+            grads_first(head, block)
+
+            @pl.when((block == 0) & (head > 0))
+            def _():
+                grads_second(head - 1)
 
             @pl.when((block == 1) & (head < HEADS - 1))
             def _():
@@ -326,25 +339,20 @@
             def _():
                 send_own(head + 2)
 
-            @pl.when((block == 2) & (head > 0))
-            def _():
-                grads_second(head - 1)
+            @pl.when((block == 2) & (head > 1))
+            def _():
+                grads_last(head - 2)
 
             return carry
 
         lax.fori_loop(0, PEERS, one_block, 0)
-        grads_first(head)
         send_back(od.at[head, 0], 2, o_out, 0, head)
         send_back(od.at[head, 1], 2, dq_out, 1, head)
-
-        @pl.when(head > 0)
-        def _():
-            grads_last(head - 1)
-
         return carry
 
     lax.fori_loop(0, HEADS, one_head, 0)
     grads_second(HEADS - 1)
+    grads_last(HEADS - 2)
     grads_last(HEADS - 1)
 
     for array, buffer in enumerate((kv, kv, qd, qd)):

time: 105 us -> 98.6 us (0.939)
  Pallas kernels: 97.6 us -> 90.9 us
    pallas_call x1, Pallas kernels: 97.6 us -> 90.9 us  [step(): pl.pallas_call(call, name='window_attention', out_shape=(jax.ShapeDtypeSt...]
where the time goes in v2:
time: 98.6 us; the launch traced here: 97.3 us
  Pallas kernels  90.9 us (92%)
  local copies, waits for them, and re-layouts  5.8 us (6%)
    pallas_call x1, Pallas kernels, step(): pl.pallas_call(call, name='window_attention', out_shape=(jax.ShapeDtypeSt...  90.9 us
    unnamed x10, local copies, waits for them, and re-layouts  5.8 us

profile of v2, /device:TPU:216, one launch (start us, length us, event | category | flops | bytes accessed | tf_op | source)
XLA Modules:
  0.0 97.3 jit_solution(4024946406620363073)
XLA Ops:
  0.6 90.9 %window_attention.1 = (bf16[128,4096]{1,0:T(8,128)(2,1)}, bf16[128,4096]{1,0:T(8,128)(2,1)}, bf16[128,2048]{1,0:T(8,128)(2,1)}, bf16[128,2048]{1,0:T(8,128)(2,1)}) custom-call(bf16[128,4096]{1,0:T(8,128)(2,1)} %refs_0_.1, bf16[128,2048]{1,0:T(8,128)(2,1)} %refs_1_.1, bf16[128,2048]{1,0:T(8,128)(2,1)} %refs_2_.1, bf16[128,4096]{1,0:T(8,128)(2,1)} %refs_3_.1), custom_call_target="tpu_custom_call" | custom-call | flops 6039797760 | bytes 12582912 | tf_op jit(solution)/shard_map/window_attention/pallas_call | solution.py:393
  91.5 0.0 copy-start
  91.5 2.4 %copy.12 = bf16[128,4096]{1,0:T(8,128)(2,1)} copy(bf16[128,4096]{1,0:T(8,128)(2,1)} %get-tuple-element.8) | data formatting | bytes 2097152
  93.9 0.0 copy-done
  93.9 0.0 copy-start.2
  93.9 1.0 copy.13
  94.9 0.4 copy-done.2
  95.3 0.0 copy-start.1
  95.3 0.8 copy.14
  96.1 0.4 copy-done.1
  96.6 0.8 copy.15
Async XLA Ops:
  91.5 2.4 %copy-start = (bf16[128,4096]{1,0:T(8,128)(2,1)S(1)}, bf16[128,4096]{1,0:T(8,128)(2,1)}, u32[]{:S(2)}) copy-start(bf16[128,4096]{1,0:T(8,128)(2,1)} %get-tuple-element.9) | copy-start | bytes 3145732
  93.9 1.4 %copy-start.2 = (bf16[128,2048]{1,0:T(8,128)(2,1)S(1)}, bf16[128,2048]{1,0:T(8,128)(2,1)}, u32[]{:S(2)}) copy-start(bf16[128,2048]{1,0:T(8,128)(2,1)} %get-tuple-element.10) | copy-start | bytes 1572868
  95.3 1.2 %copy-start.1 = (bf16[128,2048]{1,0:T(8,128)(2,1)S(1)}, bf16[128,2048]{1,0:T(8,128)(2,1)}, u32[]{:S(2)}) copy-start(bf16[128,2048]{1,0:T(8,128)(2,1)} %get-tuple-element.11) | copy-start | bytes 1572868
